TPU v7x, 32 devices: a whole 2x2x4 slice. The times are simulated.
32 devices in a mesh: section: 2 (over y), tensor: 4 (over z), dp: 4 (over x, core).
Axes of the slice: x: 2, y: 2, z: 4, core: 2. Of those that a mesh axis runs over, the one named last changes fastest.
Arguments:
- tokens_in: bfloat16 [4, 256, 4, 2048], P(None, 'tensor', 'dp'), may hold values from -6 to 6
- cotangent: bfloat16 [4, 256, 4, 2048], P(None, 'tensor', 'dp'), may hold values from -6 to 6
- ln1_gain: bfloat16 [2, 2048], P('section'), may hold values from 0.5 to 1.5
- ln1_bias: bfloat16 [2, 2048], P('section'), may hold values from -1 to 1
- q_weight: bfloat16 [2, 2048, 2048], P('section', None, 'tensor'), may hold values from -0.125 to 0.125
- q_bias: bfloat16 [2, 2048], P('section', 'tensor'), may hold values from -1.5 to 1.5
- kv_weight: bfloat16 [2, 2048, 256], P('section'), may hold values from -0.125 to 0.125
- v_bias: bfloat16 [2, 128], P('section'), may hold values from -0.25 to 0.25
- o_weight: bfloat16 [2, 2048, 2048], P('section', 'tensor'), may hold values from -1.5 to 1.5
- o_bias: bfloat16 [2, 2048], P('section'), may hold values from -1.5 to 1.5
- ln2_gain: bfloat16 [2, 2048], P('section'), may hold values from 0.5 to 1.5
- ln2_bias: bfloat16 [2, 2048], P('section'), may hold values from -1 to 1
- up_weight: bfloat16 [2, 2048, 8192], P('section', None, 'tensor'), may hold values from -0.125 to 0.125
- up_bias: bfloat16 [2, 8192], P('section', 'tensor'), may hold values from -1.5 to 1.5
- down_weight: bfloat16 [2, 8192, 2048], P('section', 'tensor'), may hold values from -0.0625 to 0.0625
- down_bias: bfloat16 [2, 2048], P('section'), may hold values from -1.5 to 1.5
Outputs:
- layer_out: bfloat16 [2, 4, 256, 4, 2048], P('section', None, 'tensor', 'dp')
- input_grad: float32 [2, 4, 256, 4, 2048], P('section', None, 'tensor', 'dp')
- ln1_gain_grad: float32 [2, 2048], P('section')
- ln1_bias_grad: float32 [2, 2048], P('section')
- q_weight_grad: float32 [2, 2048, 2048], P('section', None, 'tensor')
- q_bias_grad: float32 [2, 2048], P('section', 'tensor')
- kv_weight_grad: float32 [2, 2048, 256], P('section')
- v_bias_grad: float32 [2, 128], P('section')
- o_weight_grad: float32 [2, 2048, 2048], P('section', 'tensor')
- o_bias_grad: float32 [2, 2048], P('section')
- ln2_gain_grad: float32 [2, 2048], P('section')
- ln2_bias_grad: float32 [2, 2048], P('section')
- up_weight_grad: float32 [2, 2048, 8192], P('section', None, 'tensor')
- up_bias_grad: float32 [2, 8192], P('section', 'tensor')
- down_weight_grad: float32 [2, 8192, 2048], P('section', 'tensor')
- down_bias_grad: float32 [2, 2048], P('section')
All inputs are finite; a program needn't handle non-finite values.
Results may differ from a plain program's by a relative error of at most 0.022.
Values may be sent and summed in bfloat16 or wider, within the bound.
A program may use at most 512 MiB of HBM per device.

v0:
```python
import math
import jax
import jax.numpy as jnp
from jax import lax
from jax.sharding import PartitionSpec as P

HD = 128
F32 = jnp.float32
BF16 = jnp.bfloat16


def from_behind(block, axis, distance):
    devices = range(lax.axis_size(axis))
    route = [(i - distance, i) for i in devices if i - distance in devices]
    return lax.ppermute(block, axis, route)


def layer_norm(values, gain_vec, bias_vec):
    row_mean = jnp.mean(values, axis=-1, keepdims=True)
    centred = values - row_mean
    row_var = jnp.mean(centred * centred, axis=-1, keepdims=True)
    return centred * lax.rsqrt(row_var + 1e-05) * gain_vec + bias_vec


def gelu_tanh(values):
    return jax.nn.gelu(values, approximate=True)


def dot(a, b):
    return jnp.dot(a, b, preferred_element_type=F32)


def dot_t(a, b):
    return lax.dot_general(a, b, (((1,), (1,)), ((), ())), preferred_element_type=F32)


def t_dot(a, b):
    return lax.dot_general(a, b, (((0,), (0,)), ((), ())), preferred_element_type=F32)


def gather_rows(own_rows):
    return lax.all_gather(own_rows, "tensor", axis=0, tiled=True)


def sum_rows(partial):
    return lax.psum_scatter(partial.astype(BF16), "tensor", scatter_dimension=0, tiled=True).astype(
        F32
    )


def swap(value, distance):
    size = lax.axis_size("dp")
    return lax.ppermute(value, "dp", [(i, i ^ distance) for i in range(size)])


def fold(value, distance, axis):
    bit = lax.axis_index("dp") // distance % 2
    half = value.shape[axis] // 2
    away = lax.dynamic_slice_in_dim(value, (1 - bit) * half, half, axis)
    kept = lax.dynamic_slice_in_dim(value, bit * half, half, axis)
    return kept + swap(away.astype(BF16), distance).astype(F32)


def unfold(value, distance, axis):
    bit = lax.axis_index("dp") // distance % 2
    other = swap(value, distance)
    low = jnp.where(bit == 0, value, other)
    high = jnp.where(bit == 0, other, value)
    return jnp.concatenate([low, high], axis=axis)


def sum_dp(value, axis, scatter=None):
    size = lax.axis_size("dp")
    distance = 1
    while distance < size:
        value = fold(value, distance, axis)
        if distance == 1 and scatter is not None:
            value = lax.psum_scatter(
                value.astype(BF16), "tensor", scatter_dimension=scatter, tiled=True
            ).astype(F32)
        distance *= 2
    value = value.astype(BF16)
    while distance > 1:
        distance //= 2
        value = unfold(value, distance, axis)
    return value.astype(F32)


def whole_weight(shard, split, join):
    size = lax.axis_size("dp")
    part = shard.shape[split] // size
    own = lax.dynamic_slice_in_dim(shard, lax.axis_index("dp") * part, part, split)
    own = lax.all_gather(own, "tensor", axis=join, tiled=True)
    return lax.all_gather(own, "dp", axis=split, tiled=True)


def on_device(
    tokens_in,
    cotangent,
    ln1_gain,
    ln1_bias,
    q_weight,
    q_bias,
    kv_weight,
    v_bias,
    o_weight,
    o_bias,
    ln2_gain,
    ln2_bias,
    up_weight,
    up_bias,
    down_weight,
    down_bias,
):
    section = lax.axis_index("section")
    tensor_count = lax.axis_size("tensor")
    tensor_rank = lax.axis_index("tensor")
    gain_one = ln1_gain[0].astype(F32)
    bias_one = ln1_bias[0].astype(F32)
    w_pairs = kv_weight[0]
    pair_bias = jnp.concatenate([jnp.zeros((HD,), F32), v_bias[0].astype(F32)])
    b_out = o_bias[0].astype(F32)
    gain_two = ln2_gain[0].astype(F32)
    bias_two = ln2_bias[0].astype(F32)
    w_up = up_weight[0]
    b_up = up_bias[0].astype(F32)
    w_down = down_weight[0]
    b_down = down_bias[0].astype(F32)
    blocks, own_count, seq_count, model_dim = tokens_in.shape
    assert seq_count == 1
    tokens_in = tokens_in[:, :, 0]
    cotangent = cotangent[:, :, 0]
    block_len = own_count * tensor_count
    total_len = blocks * block_len
    w_query = whole_weight(q_weight[0], 0, 1)
    w_out = whole_weight(o_weight[0], 1, 0)
    b_query = lax.all_gather(q_bias[0], "tensor", axis=0, tiled=True).astype(F32)
    heads = w_query.shape[1] // HD
    width = heads * HD
    ff_local = w_up.shape[1]
    score_scale = 1.0 / math.sqrt(HD)
    positions = jnp.arange(total_len, dtype=jnp.int32)

    def zeros(shape, dtype):
        return jnp.zeros(shape, dtype)

    kept_normed = zeros((blocks, own_count, model_dim), BF16)
    kept_query = zeros((blocks, own_count, width), BF16)
    kept_attended = zeros((blocks, own_count, width), BF16)
    kept_logsum = zeros((blocks, own_count * heads), F32)
    kv_cache = zeros((total_len, 2 * HD), BF16)
    kept_input = zeros((blocks, own_count, model_dim), F32)
    kept_hidden = zeros((blocks, own_count, model_dim), F32)
    kept_normed_two = zeros((blocks, block_len, model_dim), BF16)
    kept_pre = zeros((blocks, block_len, ff_local), F32)
    kept_active = zeros((blocks, block_len, ff_local), BF16)
    outputs = zeros((blocks, own_count, model_dim), BF16)
    received = zeros((own_count, model_dim), F32)

    def put(kept, value, index):
        return lax.dynamic_update_index_in_dim(kept, value, index, 0)

    def take(kept, index):
        return lax.dynamic_index_in_dim(kept, index, 0, keepdims=False)

    for turn in range(blocks + 1):
        block_index = jnp.clip(turn - section, 0, blocks - 1)
        layer_input = jnp.where(section == 0, take(tokens_in, block_index).astype(F32), received)
        normed = layer_norm(layer_input, gain_one, bias_one).astype(BF16)
        pairs = gather_rows((dot(normed, w_pairs) + pair_bias).astype(BF16))
        kv_cache = lax.dynamic_update_slice_in_dim(kv_cache, pairs, block_index * block_len, 0)
        query = (dot(normed, w_query) + b_query).astype(BF16)
        visible = positions < (block_index + 1) * block_len
        query_rows = query.reshape(own_count * heads, HD)
        scores = dot_t(query_rows, kv_cache[:, :HD]) * score_scale
        scores = jnp.where(visible, scores, -1e30)
        row_top = jnp.max(scores, axis=-1, keepdims=True)
        exponent = jnp.exp(scores - row_top)
        row_total = jnp.sum(exponent, axis=-1, keepdims=True)
        log_total = (row_top + jnp.log(row_total))[:, 0]
        weights_low = (exponent / row_total).astype(BF16)
        attended = dot(weights_low, kv_cache[:, HD:]).astype(BF16).reshape(own_count, width)
        hidden = layer_input + dot(attended, w_out) + b_out
        normed_two = gather_rows(layer_norm(hidden, gain_two, bias_two).astype(BF16))
        pre_active = dot(normed_two, w_up) + b_up
        active = gelu_tanh(pre_active).astype(BF16)
        result_low = (hidden + sum_rows(dot(active, w_down)) + b_down).astype(BF16)
        kept_normed = put(kept_normed, normed, block_index)
        kept_query = put(kept_query, query, block_index)
        kept_attended = put(kept_attended, attended, block_index)
        kept_logsum = put(kept_logsum, log_total, block_index)
        kept_input = put(kept_input, layer_input, block_index)
        kept_hidden = put(kept_hidden, hidden, block_index)
        kept_normed_two = put(kept_normed_two, normed_two, block_index)
        kept_pre = put(kept_pre, pre_active, block_index)
        kept_active = put(kept_active, active, block_index)
        outputs = put(outputs, result_low, block_index)
        if turn < blocks:
            received = from_behind(result_low, "section", 1).astype(F32)
    key_rows = kv_cache[:, :HD]
    value_rows = kv_cache[:, HD:]
    kept_grad_mlp = zeros((blocks + 1, block_len, model_dim), BF16)
    kept_grad_pre = zeros((blocks + 1, block_len, ff_local), BF16)
    kept_branch = zeros((blocks + 1, own_count, model_dim), BF16)
    kept_grad_query = zeros((blocks + 1, own_count, width), BF16)
    kept_grad_pairs = zeros((blocks + 1, own_count, 2 * HD), BF16)
    input_grads = zeros((blocks + 1, own_count, model_dim), F32)
    pair_grad_acc = zeros((total_len, 2 * HD), F32)
    received_back = zeros((own_count, model_dim), F32)
    common = [zeros((model_dim,), F32) for _ in range(6)]
    for turn in range(blocks + 1):
        step_count = turn - (1 - section)
        valid = (step_count >= 0) & (step_count < blocks)
        block_index = blocks - 1 - jnp.clip(step_count, 0, blocks - 1)
        slot = jnp.where(valid, block_index, blocks)
        grad_out = jnp.where(section == 1, take(cotangent, block_index).astype(F32), received_back)
        grad_out = grad_out * valid.astype(F32)
        pre_active = take(kept_pre, block_index)
        grad_mlp = gather_rows(grad_out.astype(BF16))
        grad_active = dot_t(grad_mlp, w_down)
        grad_pre = jax.vjp(gelu_tanh, pre_active)[1](grad_active)[0].astype(BF16)
        grad_normed_two = sum_rows(dot_t(grad_pre, w_up))
        norm_back_two = jax.vjp(layer_norm, take(kept_hidden, block_index), gain_two, bias_two)[1]
        grad_hidden_norm, gain_two_term, bias_two_term = norm_back_two(grad_normed_two)
        grad_hidden = grad_out + grad_hidden_norm
        branch = grad_hidden.astype(BF16)
        grad_attended = dot_t(branch, w_out).astype(BF16).reshape(own_count * heads, HD)
        query_rows = take(kept_query, block_index).reshape(own_count * heads, HD)
        log_total = take(kept_logsum, block_index)
        visible = positions < (block_index + 1) * block_len
        scores = dot_t(query_rows, key_rows) * score_scale
        scores = jnp.where(visible, scores, -1e30)
        probabilities = jnp.exp(scores - log_total[:, None])
        grad_probs = dot_t(grad_attended, value_rows)
        row_inner = jnp.sum(probabilities * grad_probs, axis=-1, keepdims=True)
        grad_scores = (probabilities * (grad_probs - row_inner)).astype(BF16)
        grad_query = (dot(grad_scores, key_rows) * score_scale).astype(BF16)
        grad_query = grad_query.reshape(own_count, width)
        grad_keys = t_dot(grad_scores, query_rows) * score_scale
        grad_values = t_dot(probabilities.astype(BF16), grad_attended)
        pair_grad_acc = pair_grad_acc + jnp.concatenate([grad_keys, grad_values], axis=-1)
        block_pairs = lax.dynamic_slice_in_dim(pair_grad_acc, block_index * block_len, block_len, 0)
        grad_pairs = sum_rows(block_pairs).astype(BF16)
        grad_normed = dot_t(grad_query, w_query) + dot_t(grad_pairs, w_pairs)
        norm_back_one = jax.vjp(layer_norm, take(kept_input, block_index), gain_one, bias_one)[1]
        grad_input_norm, gain_one_term, bias_one_term = norm_back_one(grad_normed)
        grad_input = grad_hidden + grad_input_norm
        if turn < blocks:
            received_back = from_behind(grad_input.astype(BF16), "section", -1).astype(F32)
        scale = valid.astype(F32)
        terms = (
            gain_one_term * scale,
            bias_one_term * scale,
            jnp.sum(grad_hidden, axis=0),
            gain_two_term,
            bias_two_term,
            jnp.sum(grad_out, axis=0),
        )
        common = [total + term for total, term in zip(common, terms)]
        input_grads = put(input_grads, grad_input, slot)
        kept_grad_mlp = put(kept_grad_mlp, grad_mlp, slot)
        kept_grad_pre = put(kept_grad_pre, grad_pre, slot)
        kept_branch = put(kept_branch, branch, slot)
        kept_grad_query = put(kept_grad_query, grad_query, slot)
        kept_grad_pairs = put(kept_grad_pairs, grad_pairs, slot)

    def flat(kept):
        return kept[:blocks].reshape(-1, kept.shape[-1])

    down_w = t_dot(flat(kept_active), flat(kept_grad_mlp))
    up_w = t_dot(flat(kept_normed_two), flat(kept_grad_pre))
    up_b = jnp.sum(flat(kept_grad_pre).astype(F32), axis=0)
    out_w = t_dot(flat(kept_attended), flat(kept_branch))
    query_w = t_dot(flat(kept_normed), flat(kept_grad_query))
    query_b = jnp.sum(flat(kept_grad_query).astype(F32), axis=0)
    pair_w = t_dot(flat(kept_normed), flat(kept_grad_pairs))
    value_b = jnp.sum(flat(kept_grad_pairs)[:, HD:].astype(F32), axis=0)
    down_w = sum_dp(down_w, 0)
    up_w = sum_dp(up_w, 0)
    out_w = sum_dp(out_w, 1, 0)
    query_w = sum_dp(query_w, 0, 1)
    pair_w = lax.psum(pair_w.astype(BF16), ("tensor", "dp")).astype(F32)
    wide = jnp.zeros((tensor_count, ff_local), F32)
    wide = lax.dynamic_update_index_in_dim(wide, up_b, tensor_rank, 0)
    packed = jnp.concatenate([*common, query_b, value_b, wide.reshape(-1)])
    packed = lax.psum(packed, ("tensor", "dp"))
    vecs = packed[: 6 * model_dim].reshape(6, model_dim)
    own_query = lax.dynamic_slice_in_dim(
        packed, 6 * model_dim + tensor_rank * (width // tensor_count), width // tensor_count, 0
    )
    value_b = lax.slice_in_dim(packed, 6 * model_dim + width, 6 * model_dim + width + HD)
    own_up = lax.dynamic_slice_in_dim(
        packed, 6 * model_dim + width + HD + tensor_rank * ff_local, ff_local, 0
    )
    return (
        outputs[None, :, :, None],
        input_grads[None, :blocks, :, None],
        vecs[0][None],
        vecs[1][None],
        query_w[None],
        own_query[None],
        pair_w[None],
        value_b[None],
        out_w[None],
        vecs[2][None],
        vecs[3][None],
        vecs[4][None],
        up_w[None],
        own_up[None],
        down_w[None],
        vecs[5][None],
    )


def solution(mesh):
    placed = (
        P(None, "tensor", "dp", None),
        P(None, "tensor", "dp", None),
        P("section", None),
        P("section", None),
        P("section", None, "tensor"),
        P("section", "tensor"),
        P("section", None, None),
        P("section", None),
        P("section", "tensor", None),
        P("section", None),
        P("section", None),
        P("section", None),
        P("section", None, "tensor"),
        P("section", "tensor"),
        P("section", "tensor", None),
        P("section", None),
    )
    return jax.shard_map(
        on_device,
        mesh=mesh,
        in_specs=placed,
        out_specs=(
            P("section", None, "tensor", "dp", None),
            P("section", None, "tensor", "dp", None),
            P("section", None),
            P("section", None),
            P("section", None, "tensor"),
            P("section", "tensor"),
            P("section", None, None),
            P("section", None),
            P("section", "tensor", None),
            P("section", None),
            P("section", None),
            P("section", None),
            P("section", None, "tensor"),
            P("section", "tensor"),
            P("section", "tensor", None),
            P("section", None),
        ),
        check_vma=False,
    )
```

profile of v0, /device:TPU:1, one launch (start us, length us, event | category | flops | bytes accessed | tf_op | source)
XLA Modules:
  0.0 1809.0 jit_solution(15878004784130863771)
XLA Ops:
  11.7 46.6 %all-gather.40.cloned.1.call-done = bf16[1,512,2048]{2,1,0:T(8,128)(2,1)} async-done(((bf16[1,512,512]{2,1,0:T(8,128)(2,1)}), bf16[1,512,2048]{2,1,0:T(8,128)(2,1)}) %all-gather.40.cloned.1.call-update) | async-done | bytes 2097168 | tf_op jit(solution)/shard_map/all_gather | solution.py:93
  58.3 46.8 %all-gather.44.cloned.1.call-done = bf16[1,2048,512]{2,1,0:T(8,128)(2,1)} async-done(((bf16[1,512,512]{2,1,0:T(8,128)(2,1)}), bf16[1,2048,512]{2,1,0:T(8,128)(2,1)}) %all-gather.44.cloned.1.call-update) | async-done | bytes 2097168 | tf_op jit(solution)/shard_map/all_gather | solution.py:93
  105.3 9.3 all-gather.2
  115.5 11.1 all_gather.63
  126.7 37.5 %all-gather.42.cloned.1.call-done = bf16[1,2048,2048]{2,1,0:T(8,128)(2,1)} async-done(((bf16[1,512,2048]{2,1,0:T(8,128)(2,1)}), bf16[1,2048,2048]{2,1,0:T(8,128)(2,1)}) %all-gather.42.cloned.1.call-update) | async-done | bytes 8388624 | tf_op jit(solution)/shard_map/all_gather | solution.py:94
  174.8 49.1 %all-gather.46.cloned.1.call-done = bf16[1,2048,2048]{2,1,0:T(8,128)(2,1)} async-done(((bf16[1,2048,512]{2,1,0:T(8,128)(2,1)}), bf16[1,2048,2048]{2,1,0:T(8,128)(2,1)}) %all-gather.46.cloned.1.call-update) | async-done | bytes 8388624 | tf_op jit(solution)/shard_map/all_gather | solution.py:94
  230.4 27.2 %all-gather.20.cloned.1.call-done = bf16[256,2048]{1,0:T(8,128)(2,1)} async-done(((bf16[64,2048]{1,0:T(8,128)(2,1)}), bf16[256,2048]{1,0:T(8,128)(2,1)}) %all-gather.20.cloned.1.call-update) | async-done | bytes 1048592 | tf_op jit(solution)/shard_map/all_gather | solution.py:42
  262.1 7.2 bitcast_dynamic-update-slice_fusion.4
  274.3 26.7 %reduce-scatter.18.cloned.1.call-done = bf16[64,2048]{1,0:T(8,128)(2,1)} async-done(((bf16[256,2048]{1,0:T(8,128)(2,1)}), bf16[64,2048]{1,0:T(8,128)(2,1)}) %reduce-scatter.18.cloned.1.call-update) | async-done | bytes 262160 | tf_op jit(solution)/shard_map/reduce_scatter | solution.py:46
  312.8 11.2 all_gather.67
  342.7 30.8 %all-gather.22.cloned.1.call-done = bf16[256,2048]{1,0:T(8,128)(2,1)} async-done(((bf16[64,2048]{1,0:T(8,128)(2,1)}), bf16[256,2048]{1,0:T(8,128)(2,1)}) %all-gather.22.cloned.1.call-update) | async-done | bytes 1048592 | tf_op jit(solution)/shard_map/all_gather | solution.py:42
  373.4 7.4 bitcast_dynamic-update-slice_fusion.3
  389.1 26.7 %reduce-scatter.20.cloned.1.call-done = bf16[64,2048]{1,0:T(8,128)(2,1)} async-done(((bf16[256,2048]{1,0:T(8,128)(2,1)}), bf16[64,2048]{1,0:T(8,128)(2,1)}) %reduce-scatter.20.cloned.1.call-update) | async-done | bytes 262160 | tf_op jit(solution)/shard_map/reduce_scatter | solution.py:46
  426.6 11.2 all_gather.69
  456.2 31.1 %all-gather.24.cloned.1.call-done = bf16[256,2048]{1,0:T(8,128)(2,1)} async-done(((bf16[64,2048]{1,0:T(8,128)(2,1)}), bf16[256,2048]{1,0:T(8,128)(2,1)}) %all-gather.24.cloned.1.call-update) | async-done | bytes 1048592 | tf_op jit(solution)/shard_map/all_gather | solution.py:42
  487.3 7.4 bitcast_dynamic-update-slice_fusion.2
  502.9 26.7 %reduce-scatter.22.cloned.1.call-done = bf16[64,2048]{1,0:T(8,128)(2,1)} async-done(((bf16[256,2048]{1,0:T(8,128)(2,1)}), bf16[64,2048]{1,0:T(8,128)(2,1)}) %reduce-scatter.22.cloned.1.call-update) | async-done | bytes 262160 | tf_op jit(solution)/shard_map/reduce_scatter | solution.py:46
  540.4 11.2 all_gather.71
  570.0 31.0 %all-gather.26.cloned.1.call-done = bf16[256,2048]{1,0:T(8,128)(2,1)} async-done(((bf16[64,2048]{1,0:T(8,128)(2,1)}), bf16[256,2048]{1,0:T(8,128)(2,1)}) %all-gather.26.cloned.1.call-update) | async-done | bytes 1048592 | tf_op jit(solution)/shard_map/all_gather | solution.py:42
  601.1 7.4 bitcast_dynamic-update-slice_fusion.1
  616.7 26.7 %reduce-scatter.24.cloned.1.call-done = bf16[64,2048]{1,0:T(8,128)(2,1)} async-done(((bf16[256,2048]{1,0:T(8,128)(2,1)}), bf16[64,2048]{1,0:T(8,128)(2,1)}) %reduce-scatter.24.cloned.1.call-update) | async-done | bytes 262160 | tf_op jit(solution)/shard_map/reduce_scatter | solution.py:46
  654.3 10.5 all_gather.73
  702.6 9.3 all-gather.28.cloned.1.call-done
  711.8 8.1 bitcast_dynamic-update-slice_fusion
  719.9 20.8 %all-gather.30.cloned.1.call-done = bf16[256,2048]{1,0:T(8,128)(2,1)} async-done(((bf16[64,2048]{1,0:T(8,128)(2,1)}), bf16[256,2048]{1,0:T(8,128)(2,1)}) %all-gather.30.cloned.1.call-update) | async-done | bytes 1048592 | tf_op jit(solution)/shard_map/all_gather | solution.py:42
  744.0 8.5 bitcast_dynamic-update-slice_fusion.14
  762.3 20.4 %reduce-scatter.28.cloned.1.call-done = bf16[64,2048]{1,0:T(8,128)(2,1)} async-done(((bf16[256,2048]{1,0:T(8,128)(2,1)}), bf16[64,2048]{1,0:T(8,128)(2,1)}) %reduce-scatter.28.cloned.1.call-update) | async-done | bytes 262160 | tf_op jit(solution)/shard_map/reduce_scatter | solution.py:46
  840.3 28.2 %all-gather.32.cloned.1.call-done = bf16[256,2048]{1,0:T(8,128)(2,1)} async-done(((bf16[64,2048]{1,0:T(8,128)(2,1)}), bf16[256,2048]{1,0:T(8,128)(2,1)}) %all-gather.32.cloned.1.call-update) | async-done | bytes 1048592 | tf_op jit(solution)/shard_map/all_gather | solution.py:42
  868.5 8.6 bitcast_dynamic-update-slice_fusion.13
  889.5 21.2 %reduce-scatter.32.cloned.1.call-done = bf16[64,2048]{1,0:T(8,128)(2,1)} async-done(((bf16[256,2048]{1,0:T(8,128)(2,1)}), bf16[64,2048]{1,0:T(8,128)(2,1)}) %reduce-scatter.32.cloned.1.call-update) | async-done | bytes 262160 | tf_op jit(solution)/shard_map/reduce_scatter | solution.py:46
  967.2 28.4 %all-gather.34.cloned.1.call-done = bf16[256,2048]{1,0:T(8,128)(2,1)} async-done(((bf16[64,2048]{1,0:T(8,128)(2,1)}), bf16[256,2048]{1,0:T(8,128)(2,1)}) %all-gather.34.cloned.1.call-update) | async-done | bytes 1048592 | tf_op jit(solution)/shard_map/all_gather | solution.py:42
  995.6 8.6 bitcast_dynamic-update-slice_fusion.12
  1016.6 21.2 %reduce-scatter.36.cloned.1.call-done = bf16[64,2048]{1,0:T(8,128)(2,1)} async-done(((bf16[256,2048]{1,0:T(8,128)(2,1)}), bf16[64,2048]{1,0:T(8,128)(2,1)}) %reduce-scatter.36.cloned.1.call-update) | async-done | bytes 262160 | tf_op jit(solution)/shard_map/reduce_scatter | solution.py:46
  1122.7 8.6 bitcast_dynamic-update-slice_fusion.11
  1240.0 10.0 all-gather.38.cloned.1.call-done
  1250.0 8.6 bitcast_dynamic-update-slice_fusion.10
  1347.3 18.3 %convolution_bitcast_fusion = f32[2048,2048]{1,0:T(8,128)} fusion(bf16[4,256,2048]{1,2,0:T(8,128)(2,1)} %get-tuple-element.221, bf16[5,256,2048]{2,1,0:T(8,128)(2,1)} %bitcast_dynamic-update-slice_fusion.5), kind=kOutput, calls=%fused_computation | convolution fusion | flops 8589934592 | bytes 25165824 | tf_op jit(solution)/shard_map/dot_general | solution.py:38
  1398.4 8.4 add_convert_fusion.1
  1406.9 12.6 convolution_bitcast_fusion.1
  1464.0 41.4 %collective-permute-done.21 = bf16[512,2048]{1,0:T(8,128)(2,1)} collective-permute-done((bf16[512,2048]{1,0:T(8,128)(2,1)}, bf16[512,2048]{1,0:T(8,128)(2,1)}, u32[]{:S(2)}, u32[]{:S(2)}) %collective-permute-start.21) | collective-permute-done | bytes 2097184 | tf_op jit(solution)/shard_map/ppermute | solution.py:53
  1511.4 8.3 add_convert_fusion
  1522.4 29.8 %collective-permute-done.17 = bf16[512,2048]{1,0:T(8,128)(2,1)} collective-permute-done((bf16[512,2048]{1,0:T(8,128)(2,1)}, bf16[512,2048]{1,0:T(8,128)(2,1)}, u32[]{:S(2)}, u32[]{:S(2)}) %collective-permute-start.17) | collective-permute-done | bytes 2097184 | tf_op jit(solution)/shard_map/ppermute | solution.py:53
  1557.1 43.0 %collective-permute-done.22 = bf16[512,2048]{1,0:T(8,128)(2,1)} collective-permute-done((bf16[512,2048]{1,0:T(8,128)(2,1)}, bf16[512,2048]{1,0:T(8,128)(2,1)}, u32[]{:S(2)}, u32[]{:S(2)}) %collective-permute-start.22) | collective-permute-done | bytes 2097184 | tf_op jit(solution)/shard_map/ppermute | solution.py:53
  1608.0 37.0 %collective-permute-done.18 = bf16[512,2048]{1,0:T(8,128)(2,1)S(1)} collective-permute-done((bf16[512,2048]{1,0:T(8,128)(2,1)S(1)}, bf16[512,2048]{1,0:T(8,128)(2,1)S(1)}, u32[]{:S(2)}, u32[]{:S(2)}) %collective-permute-start.18) | collective-permute-done | bytes 2097184 | tf_op jit(solution)/shard_map/ppermute | solution.py:53
  1669.2 68.0 %reduce-scatter.50.cloned.1.call-done = bf16[512,1024]{1,0:T(8,128)(2,1)} async-done(((bf16[2048,1024]{1,0:T(8,128)(2,1)}), bf16[512,1024]{1,0:T(8,128)(2,1)}) %reduce-scatter.50.cloned.1.call-update) | async-done | bytes 1048592 | tf_op jit(solution)/shard_map/reduce_scatter | solution.py:78
  1740.8 11.8 maximum_convert_fusion.1
  1770.3 7.8 collective-permute-done.14
  1781.1 11.8 maximum_convert_fusion
  (882 shorter events, 781.7 us)
Async XLA Ops:
  7.3 51.0 %all-gather.40.cloned.1.call-start = ((), (), s32[]{:S(2)}) async-start(), calls=%async_computation.46 | async-start | bytes 2621440 | tf_op jit(solution)/shard_map/all_gather | solution.py:93
  9.6 95.5 %all-gather.44.cloned.1.call-start = ((), (), s32[]{:S(2)}) async-start(), calls=%async_computation.48 | async-start | bytes 2621440 | tf_op jit(solution)/shard_map/all_gather | solution.py:93
  11.7 152.5 %all-gather.42.cloned.1.call-start = ((), (), s32[]{:S(2)}) async-start(), calls=%async_computation.47 | async-start | bytes 10485760 | tf_op jit(solution)/shard_map/all_gather | solution.py:94
  58.3 165.6 %all-gather.46.cloned.1.call-start = ((), (), s32[]{:S(2)}) async-start(), calls=%async_computation.49 | async-start | bytes 10485760 | tf_op jit(solution)/shard_map/all_gather | solution.py:94
  105.2 152.5 %all-gather.20.cloned.1.call-start = ((), (), s32[]{:S(2)}) async-start(), calls=%async_computation.17 | async-start | bytes 1310720 | tf_op jit(solution)/shard_map/all_gather | solution.py:42
  230.1 70.8 %reduce-scatter.18.cloned.1.call-start = ((), (), s32[]{:S(2)}) async-start(), calls=%async_computation.18 | async-start | bytes 1310720 | tf_op jit(solution)/shard_map/reduce_scatter | solution.py:46
  274.2 99.2 %all-gather.22.cloned.1.call-start = ((), (), s32[]{:S(2)}) async-start(), calls=%async_computation.19 | async-start | bytes 1310720 | tf_op jit(solution)/shard_map/all_gather | solution.py:42
  342.2 73.6 %reduce-scatter.20.cloned.1.call-start = ((), (), s32[]{:S(2)}) async-start(), calls=%async_computation.20 | async-start | bytes 1310720 | tf_op jit(solution)/shard_map/reduce_scatter | solution.py:46
  389.0 98.2 %all-gather.24.cloned.1.call-start = ((), (), s32[]{:S(2)}) async-start(), calls=%async_computation.21 | async-start | bytes 1310720 | tf_op jit(solution)/shard_map/all_gather | solution.py:42
  456.0 73.7 %reduce-scatter.22.cloned.1.call-start = ((), (), s32[]{:S(2)}) async-start(), calls=%async_computation.22 | async-start | bytes 1310720 | tf_op jit(solution)/shard_map/reduce_scatter | solution.py:46
  502.9 98.2 %all-gather.26.cloned.1.call-start = ((), (), s32[]{:S(2)}) async-start(), calls=%async_computation.23 | async-start | bytes 1310720 | tf_op jit(solution)/shard_map/all_gather | solution.py:42
  569.8 73.7 %reduce-scatter.24.cloned.1.call-start = ((), (), s32[]{:S(2)}) async-start(), calls=%async_computation.24 | async-start | bytes 1310720 | tf_op jit(solution)/shard_map/reduce_scatter | solution.py:46
  616.7 95.2 %all-gather.28.cloned.1.call-start = ((), (), s32[]{:S(2)}) async-start(), calls=%async_computation.25 | async-start | bytes 1310720 | tf_op jit(solution)/shard_map/all_gather | solution.py:42
  680.6 60.1 %all-gather.30.cloned.1.call-start = ((), (), s32[]{:S(2)}) async-start(), calls=%async_computation.27 | async-start | bytes 1310720 | tf_op jit(solution)/shard_map/all_gather | solution.py:42
  683.0 99.7 %reduce-scatter.28.cloned.1.call-start = ((), (), s32[]{:S(2)}) async-start(), calls=%async_computation.28 | async-start | bytes 1310720 | tf_op jit(solution)/shard_map/reduce_scatter | solution.py:46
  755.9 68.3 %reduce-scatter.30.cloned.1.call-start = ((), (), s32[]{:S(2)}) async-start(), calls=%async_computation.29 | async-start | bytes 163840 | tf_op jit(solution)/shard_map/reduce_scatter | solution.py:46
  808.3 60.2 %all-gather.32.cloned.1.call-start = ((), (), s32[]{:S(2)}) async-start(), calls=%async_computation.30 | async-start | bytes 1310720 | tf_op jit(solution)/shard_map/all_gather | solution.py:42
  839.8 70.8 %reduce-scatter.32.cloned.1.call-start = ((), (), s32[]{:S(2)}) async-start(), calls=%async_computation.31 | async-start | bytes 1310720 | tf_op jit(solution)/shard_map/reduce_scatter | solution.py:46
  883.9 68.3 %reduce-scatter.34.cloned.1.call-start = ((), (), s32[]{:S(2)}) async-start(), calls=%async_computation.32 | async-start | bytes 163840 | tf_op jit(solution)/shard_map/reduce_scatter | solution.py:46
  936.3 59.3 %all-gather.34.cloned.1.call-start = ((), (), s32[]{:S(2)}) async-start(), calls=%async_computation.33 | async-start | bytes 1310720 | tf_op jit(solution)/shard_map/all_gather | solution.py:42
  967.0 70.8 %reduce-scatter.36.cloned.1.call-start = ((), (), s32[]{:S(2)}) async-start(), calls=%async_computation.34 | async-start | bytes 1310720 | tf_op jit(solution)/shard_map/reduce_scatter | solution.py:46
  1011.0 68.3 %reduce-scatter.38.cloned.1.call-start = ((), (), s32[]{:S(2)}) async-start(), calls=%async_computation.35 | async-start | bytes 163840 | tf_op jit(solution)/shard_map/reduce_scatter | solution.py:46
  1063.4 59.3 %all-gather.36.cloned.1.call-start = ((), (), s32[]{:S(2)}) async-start(), calls=%async_computation.36 | async-start | bytes 1310720 | tf_op jit(solution)/shard_map/all_gather | solution.py:42
  1094.1 70.8 %reduce-scatter.40.cloned.1.call-start = ((), (), s32[]{:S(2)}) async-start(), calls=%async_computation.37 | async-start | bytes 1310720 | tf_op jit(solution)/shard_map/reduce_scatter | solution.py:46
  1138.1 68.3 %reduce-scatter.42.cloned.1.call-start = ((), (), s32[]{:S(2)}) async-start(), calls=%async_computation.38 | async-start | bytes 163840 | tf_op jit(solution)/shard_map/reduce_scatter | solution.py:46
  1190.6 59.4 %all-gather.38.cloned.1.call-start = ((), (), s32[]{:S(2)}) async-start(), calls=%async_computation.39 | async-start | bytes 1310720 | tf_op jit(solution)/shard_map/all_gather | solution.py:42
  1221.3 70.8 %reduce-scatter.44.cloned.1.call-start = ((), (), s32[]{:S(2)}) async-start(), calls=%async_computation.40 | async-start | bytes 1310720 | tf_op jit(solution)/shard_map/reduce_scatter | solution.py:46
  1265.4 118.9 %reduce-scatter.46.cloned.1.call-start = ((), (), s32[]{:S(2)}) async-start(), calls=%async_computation.41 | async-start | bytes 163840 | tf_op jit(solution)/shard_map/reduce_scatter | solution.py:46
  1314.2 205.5 %reduce-scatter.26.cloned.1.call-start = ((), (), s32[]{:S(2)}) async-start(), calls=%async_computation.26 | async-start | bytes 1310720 | tf_op jit(solution)/shard_map/reduce_scatter | solution.py:46
  1321.3 331.7 %all-reduce.4.cloned.1.call-start = ((), (), s32[]{:S(2)}) async-start(), calls=%async_computation.42 | async-start | bytes 188416 | tf_op jit(solution)/shard_map/psum | solution.py:286
  1346.4 52.0 %collective-permute-start.8 = (bf16[1024,2048]{1,0:T(8,128)(2,1)}, bf16[1024,2048]{1,0:T(8,128)(2,1)}, u32[]{:S(2)}, u32[]{:S(2)}) collective-permute-start(bf16[1024,2048]{1,0:T(8,128)(2,1)} %dynamic-slice_convert_fusion.3), channel_id=1, source_target_pairs={{0,1},{1,0},{2,3},{3,2},{4,5},{5,4},{6,7},{7,6},{8,9},{9,8},{10,11... | collective-permute-start | bytes 12582920 | tf_op jit(solution)/shard_map/ppermute | solution.py:53
  1374.7 69.2 %collective-permute-start.20 = (bf16[1024,2048]{1,0:T(8,128)(2,1)}, bf16[1024,2048]{1,0:T(8,128)(2,1)}, u32[]{:S(2)}, u32[]{:S(2)}) collective-permute-start(bf16[1024,2048]{1,0:T(8,128)(2,1)} %dynamic-slice_convert_fusion), channel_id=1, source_target_pairs={{0,1},{1,0},{2,3},{3,2},{4,5},{5,4},{6,7},{7,6},{8,9},{9,8},{10,11... | collective-permute-start | bytes 12582920 | tf_op jit(solution)/shard_map/ppermute | solution.py:53
  1395.6 261.4 %all-reduce.6.cloned.1.call-start = ((), (), s32[]{:S(2)}) async-start(), calls=%async_computation.44 | async-start | bytes 2097152 | tf_op jit(solution)/shard_map/psum | solution.py:282
  1398.3 267.7 %reduce-scatter.48.cloned.1.call-start = ((), (), s32[]{:S(2)}) async-start(), calls=%async_computation.43 | async-start | bytes 5242880 | tf_op jit(solution)/shard_map/reduce_scatter | solution.py:78
  1406.8 330.3 %reduce-scatter.50.cloned.1.call-start = ((), (), s32[]{:S(2)}) async-start(), calls=%async_computation.45 | async-start | bytes 5242880 | tf_op jit(solution)/shard_map/reduce_scatter | solution.py:78
  1428.2 27.6 %collective-permute-start.16 = (bf16[1024,2048]{1,0:T(8,128)(2,1)}, bf16[1024,2048]{1,0:T(8,128)(2,1)}, u32[]{:S(2)}, u32[]{:S(2)}) collective-permute-start(bf16[1024,2048]{1,0:T(8,128)(2,1)} %dynamic-slice_convert_fusion.1), channel_id=1, source_target_pairs={{0,1},{1,0},{2,3},{3,2},{4,5},{5,4},{6,7},{7,6},{8,9},{9,8},{10,11... | collective-permute-start | bytes 12582920 | tf_op jit(solution)/shard_map/ppermute | solution.py:53
  1443.4 68.0 %collective-permute-start.12 = (bf16[2048,1024]{1,0:T(8,128)(2,1)}, bf16[2048,1024]{1,0:T(8,128)(2,1)}, u32[]{:S(2)}, u32[]{:S(2)}) collective-permute-start(bf16[2048,1024]{1,0:T(8,128)(2,1)} %dynamic-slice_convert_fusion.2), channel_id=1, source_target_pairs={{0,1},{1,0},{2,3},{3,2},{4,5},{5,4},{6,7},{7,6},{8,9},{9,8},{10,11... | collective-permute-start | bytes 12582920 | tf_op jit(solution)/shard_map/ppermute | solution.py:53
  1454.7 50.7 %collective-permute-start.21 = (bf16[512,2048]{1,0:T(8,128)(2,1)}, bf16[512,2048]{1,0:T(8,128)(2,1)}, u32[]{:S(2)}, u32[]{:S(2)}) collective-permute-start(bf16[512,2048]{1,0:T(8,128)(2,1)} %dynamic-slice_convert_fusion.4), channel_id=1, source_target_pairs={{0,2},{1,3},{2,0},{3,1},{4,6},{5,7},{6,4},{7,5},{8,10},{9,11},{10,... | collective-permute-start | bytes 6291464 | tf_op jit(solution)/shard_map/ppermute | solution.py:53
  1463.7 88.6 %collective-permute-start.17 = (bf16[512,2048]{1,0:T(8,128)(2,1)}, bf16[512,2048]{1,0:T(8,128)(2,1)}, u32[]{:S(2)}, u32[]{:S(2)}) collective-permute-start(bf16[512,2048]{1,0:T(8,128)(2,1)} %dynamic-slice_convert_fusion.5), channel_id=1, source_target_pairs={{0,2},{1,3},{2,0},{3,1},{4,6},{5,7},{6,4},{7,5},{8,10},{9,11},{10,... | collective-permute-start | bytes 6291464 | tf_op jit(solution)/shard_map/ppermute | solution.py:53
  1510.3 89.7 %collective-permute-start.22 = (bf16[512,2048]{1,0:T(8,128)(2,1)}, bf16[512,2048]{1,0:T(8,128)(2,1)}, u32[]{:S(2)}, u32[]{:S(2)}) collective-permute-start(bf16[512,2048]{1,0:T(8,128)(2,1)} %add_convert_fusion.2), channel_id=1, source_target_pairs={{0,2},{1,3},{2,0},{3,1},{4,6},{5,7},{6,4},{7,5},{8,10},{9,11},{10,... | collective-permute-start | bytes 6291464 | tf_op jit(solution)/shard_map/ppermute | solution.py:53
  1555.9 89.1 %collective-permute-start.18 = (bf16[512,2048]{1,0:T(8,128)(2,1)S(1)}, bf16[512,2048]{1,0:T(8,128)(2,1)S(1)}, u32[]{:S(2)}, u32[]{:S(2)}) collective-permute-start(bf16[512,2048]{1,0:T(8,128)(2,1)S(1)} %add_convert_fusion.3), channel_id=1, source_target_pairs={{0,2},{1,3},{2,0},{3,1},{4,6},{5,7},{6,4},{7,5},{8,10},{9,11},{10,... | collective-permute-start | bytes 6291464 | tf_op jit(solution)/shard_map/ppermute | solution.py:53
  1606.0 53.9 %collective-permute-start.23 = (bf16[1024,2048]{1,0:T(8,128)(2,1)}, bf16[1024,2048]{1,0:T(8,128)(2,1)}, u32[]{:S(2)}, u32[]{:S(2)}) collective-permute-start(bf16[1024,2048]{1,0:T(8,128)(2,1)} %pad_maximum_fusion.1), channel_id=1, source_target_pairs={{0,1},{1,0},{2,3},{3,2},{4,5},{5,4},{6,7},{7,6},{8,9},{9,8},{10,11... | collective-permute-start | bytes 12582920 | tf_op jit(solution)/shard_map/ppermute | solution.py:53
  1648.8 108.6 %collective-permute-start.19 = (bf16[1024,2048]{1,0:T(8,128)(2,1)}, bf16[1024,2048]{1,0:T(8,128)(2,1)}, u32[]{:S(2)}, u32[]{:S(2)}) collective-permute-start(bf16[1024,2048]{1,0:T(8,128)(2,1)} %pad_maximum_fusion), channel_id=1, source_target_pairs={{0,1},{1,0},{2,3},{3,2},{4,5},{5,4},{6,7},{7,6},{8,9},{9,8},{10,11... | collective-permute-start | bytes 12582920 | tf_op jit(solution)/shard_map/ppermute | solution.py:53
  1667.9 84.7 %collective-permute-start.9 = (bf16[512,512]{1,0:T(8,128)(2,1)S(1)}, bf16[512,512]{1,0:T(8,128)(2,1)S(1)}, u32[]{:S(2)}, u32[]{:S(2)}) collective-permute-start(bf16[512,512]{1,0:T(8,128)(2,1)S(1)} %dynamic-slice_convert_fusion.7), channel_id=1, source_target_pairs={{0,2},{1,3},{2,0},{3,1},{4,6},{5,7},{6,4},{7,5},{8,10},{9,11},{10,... | collective-permute-start | bytes 1572872 | tf_op jit(solution)/shard_map/ppermute | solution.py:53
  1739.6 15.2 collective-permute-start.13
  1756.3 21.7 %collective-permute-start.14 = (bf16[512,512]{1,0:T(8,128)(2,1)S(1)}, bf16[512,512]{1,0:T(8,128)(2,1)S(1)}, u32[]{:S(2)}, u32[]{:S(2)}) collective-permute-start(bf16[512,512]{1,0:T(8,128)(2,1)S(1)} %add_convert_fusion.4), channel_id=1, source_target_pairs={{0,2},{1,3},{2,0},{3,1},{4,6},{5,7},{6,4},{7,5},{8,10},{9,11},{10,... | collective-permute-start | bytes 1572872 | tf_op jit(solution)/shard_map/ppermute | solution.py:53
  1767.0 26.0 %collective-permute-start.11 = (bf16[1024,512]{1,0:T(8,128)(2,1)S(1)}, bf16[1024,512]{1,0:T(8,128)(2,1)}, u32[]{:S(2)}, u32[]{:S(2)}) collective-permute-start(bf16[1024,512]{1,0:T(8,128)(2,1)S(1)} %pad_maximum_fusion.3), channel_id=1, source_target_pairs={{0,1},{1,0},{2,3},{3,2},{4,5},{5,4},{6,7},{7,6},{8,9},{9,8},{10,11... | collective-permute-start | bytes 3145736 | tf_op jit(solution)/shard_map/ppermute | solution.py:53
  1779.3 17.9 collective-permute-start.15
  (182 other events, 3036.3 us)
Sparse Core Ops, SparseCore 0:
  10.3 47.9 all-gather.39
  60.4 44.6 all-gather.43
  106.7 57.4 all-gather.41
  165.6 58.2 all-gather.45
  230.3 27.3 all-gather.19
  274.3 26.6 reduce-scatter.17
  342.3 31.0 all-gather.21
  389.1 26.5 reduce-scatter.19
  456.1 31.1 all-gather.23
  503.0 26.6 reduce-scatter.21
  569.9 31.1 all-gather.25
  616.8 26.5 reduce-scatter.23
  680.7 31.0 all-gather.27
  713.3 27.4 all-gather.29
  756.1 26.6 reduce-scatter.27
  808.5 15.7 reduce-scatter.29
  840.0 28.5 all-gather.31
  884.0 26.6 reduce-scatter.31
  936.5 15.6 reduce-scatter.33
  967.1 28.4 all-gather.33
  1011.1 26.6 reduce-scatter.35
  1063.5 15.7 reduce-scatter.37
  1094.2 28.5 all-gather.35
  1138.2 26.6 reduce-scatter.39
  1190.7 15.6 reduce-scatter.41
  1221.4 28.5 all-gather.37
  1265.5 26.6 reduce-scatter.43
  1314.3 15.6 reduce-scatter.45
  1332.3 27.4 reduce-scatter.25
  1395.7 84.6 all-reduce.3
  1483.8 93.2 all-reduce.5
  1580.0 76.9 reduce-scatter.47
  1659.8 77.2 reduce-scatter.49
where the time goes:
time: 1820 us; the launch traced here: 1810 us
  waiting for transfers between devices  880 us (48%)
  matrix products  387 us (21%)
  other arithmetic  224 us (12%)
  local copies, waits for them, and re-layouts  197 us (11%)
  blocking collectives  64.5 us (4%)
  starting transfers between devices  38.8 us (2%)
    all_gather x10, waiting for transfers between devices, gather_rows(): return lax.all_gather(own_rows, 'tensor', axis=0, tiled=True)  222 us
    reduce_scatter x15, waiting for transfers between devices, sum_rows(): lax.psum_scatter(partial.astype(BF16), 'tensor', scatter_dimension=0, til...  205 us
    dot_general x40, matrix products, dot_t(): lax.dot_general(a, b, (((1,), (1,)), ((), ())), preferred_element_type=F32)  185 us
    ppermute x16, waiting for transfers between devices, swap(): return lax.ppermute(value, 'dp', [(i, i ^ distance) for i in range(size)])  162 us
    dot_general x35, matrix products, dot(): return jnp.dot(a, b, preferred_element_type=F32)  141 us
    all_gather x2, waiting for transfers between devices, whole_weight(): own = lax.all_gather(own, 'tensor', axis=join, tiled=True)  93.4 us
    all_gather x2, waiting for transfers between devices, whole_weight(): return lax.all_gather(own, 'dp', axis=split, tiled=True)  86.6 us
    reduce_scatter x2, waiting for transfers between devices, sum_dp(): lax.psum_scatter(value.astype(BF16), 'tensor', scatter_dimension=scatter,...  68 us
  transfers between devices with their start and end apart: 57, of which 42 were waited for; matrix products, arithmetic and copies ran while one was open for 22% of the time, Pallas kernels for 0%

commit v1 on v0

--- a/solution.py
+++ b/solution.py
@@ -9,6 +9,32 @@
 BF16 = jnp.bfloat16
 
 
+def search_forms(arr_in, bus_axis):
+    h_now, raw_out, big = (
+        jax.lax.axis_size(bus_axis),
+        jax.lax.axis_index(bus_axis),
+        arr_in.shape[0],
+    )
+    s_next = lax.dynamic_update_slice_in_dim(
+        jnp.zeros([p * h_now if ix == 0 else p for ix, p in enumerate(arr_in.shape)], arr_in.dtype),
+        arr_in,
+        raw_out * big,
+        axis=0,
+    )
+    last = response = arr_in
+    for k0 in range(1, h_now // 2 + 1):
+        last = jax.lax.ppermute(last, bus_axis, [(ix, (ix + 1) % h_now) for ix in range(h_now)])
+        s_next = lax.dynamic_update_slice_in_dim(s_next, last, (raw_out - k0) % h_now * big, axis=0)
+        if 2 * k0 < h_now:
+            response = jax.lax.ppermute(
+                response, bus_axis, [(ix, (ix - 1) % h_now) for ix in range(h_now)]
+            )
+            s_next = lax.dynamic_update_slice_in_dim(
+                s_next, response, (raw_out + k0) % h_now * big, axis=0
+            )
+    return s_next
+
+
 def from_behind(block, axis, distance):
     devices = range(lax.axis_size(axis))
     route = [(i - distance, i) for i in devices if i - distance in devices]
@@ -39,7 +65,7 @@
 
 
 def gather_rows(own_rows):
-    return lax.all_gather(own_rows, "tensor", axis=0, tiled=True)
+    return search_forms(own_rows, "tensor")
 
 
 def sum_rows(partial):

time: 1820 us -> 1750 us (0.962)
  waiting for transfers between devices: 880 us -> 779 us
  blocking collectives: 64.5 us -> 9.28 us
  starting transfers between devices: 38.8 us -> 90.7 us
  local copies, waits for them, and re-layouts: 197 us -> 239 us
    all_gather x10 -> x0, waiting for transfers between devices: 222 us -> none  [gather_rows(): return lax.all_gather(own_rows, 'tensor', axis=0, tiled=True)]
    ppermute x0 -> x45, waiting for transfers between devices: none -> 115 us  [the longest x30 93 us: search_forms(): jax.lax.ppermute(last, bus_axis, [(ix, (ix + 1) % h_now) for ix in range(...]
    all_gather x5 -> x0, blocking collectives: 55.3 us -> none  [gather_rows(): return lax.all_gather(own_rows, 'tensor', axis=0, tiled=True)]
    ppermute x0 -> x45, starting transfers between devices: none -> 51.4 us  [the longest x15 47.8 us: search_forms(): jax.lax.ppermute(response, bus_axis, [(ix, (ix - 1) % h_now) for ix in ra...]
    dynamic_update_slice x0 -> x44, local copies, waits for them, and re-layouts: none -> 27.4 us  [the longest x29 18 us: search_forms(): lax.dynamic_update_slice_in_dim(s_next, last, (raw_out - k0) % h_now * bi...]
    reduce_scatter x15, waiting for transfers between devices: 205 us -> 225 us  [sum_rows(): lax.psum_scatter(partial.astype(BF16), 'tensor', scatter_dimension=0, til...]
    unnamed x349 -> x429, local copies, waits for them, and re-layouts: 43.3 us -> 49.1 us
    dynamic_update_slice x39 -> x40, local copies, waits for them, and re-layouts: 43.1 us -> 41.6 us  [put(): return lax.dynamic_update_index_in_dim(kept, value, index, 0)]
  transfers between devices with their start and end apart: 57 -> 92, of which waited for: 42 -> 56; matrix products, arithmetic and copies ran while one was open for 22% -> 27% of each run, Pallas kernels for 0% -> 0%
where the time goes in v1:
time: 1750 us; the launch traced here: 1740 us
  waiting for transfers between devices  779 us (45%)
  matrix products  389 us (22%)
  local copies, waits for them, and re-layouts  239 us (14%)
  other arithmetic  219 us (13%)
  starting transfers between devices  90.7 us (5%)
  between operations  18 us (1%)
    reduce_scatter x15, waiting for transfers between devices, sum_rows(): lax.psum_scatter(partial.astype(BF16), 'tensor', scatter_dimension=0, til...  225 us
    dot_general x40, matrix products, dot_t(): lax.dot_general(a, b, (((1,), (1,)), ((), ())), preferred_element_type=F32)  195 us
    ppermute x16, waiting for transfers between devices, swap(): return lax.ppermute(value, 'dp', [(i, i ^ distance) for i in range(size)])  161 us
    dot_general x35, matrix products, dot(): return jnp.dot(a, b, preferred_element_type=F32)  140 us
    all_gather x2, waiting for transfers between devices, whole_weight(): own = lax.all_gather(own, 'tensor', axis=join, tiled=True)  93.3 us
    ppermute x30, waiting for transfers between devices, search_forms(): jax.lax.ppermute(last, bus_axis, [(ix, (ix + 1) % h_now) for ix in range(...  93 us
    all_gather x2, waiting for transfers between devices, whole_weight(): return lax.all_gather(own, 'dp', axis=split, tiled=True)  89.7 us
    reduce_scatter x2, waiting for transfers between devices, sum_dp(): lax.psum_scatter(value.astype(BF16), 'tensor', scatter_dimension=scatter,...  68.3 us
  transfers between devices with their start and end apart: 92, of which 56 were waited for; matrix products, arithmetic and copies ran while one was open for 27% of the time, Pallas kernels for 0%

profile of v1, /device:TPU:1, one launch (start us, length us, event | category | flops | bytes accessed | tf_op | source)
XLA Modules:
  0.0 1743.7 jit_solution(18040095591800715280)
XLA Ops:
  11.7 46.5 %all-gather.10.cloned.1.call-done = bf16[1,512,2048]{2,1,0:T(8,128)(2,1)} async-done(((bf16[1,512,512]{2,1,0:T(8,128)(2,1)}), bf16[1,512,2048]{2,1,0:T(8,128)(2,1)}) %all-gather.10.cloned.1.call-update) | async-done | bytes 2097168 | tf_op jit(solution)/shard_map/all_gather | solution.py:119
  58.3 46.8 %all-gather.14.cloned.1.call-done = bf16[1,2048,512]{2,1,0:T(8,128)(2,1)} async-done(((bf16[1,512,512]{2,1,0:T(8,128)(2,1)}), bf16[1,2048,512]{2,1,0:T(8,128)(2,1)}) %all-gather.14.cloned.1.call-update) | async-done | bytes 2097168 | tf_op jit(solution)/shard_map/all_gather | solution.py:119
  109.4 9.3 all-gather.2
  123.5 40.6 %all-gather.12.cloned.1.call-done = bf16[1,2048,2048]{2,1,0:T(8,128)(2,1)} async-done(((bf16[1,512,2048]{2,1,0:T(8,128)(2,1)}), bf16[1,2048,2048]{2,1,0:T(8,128)(2,1)}) %all-gather.12.cloned.1.call-update) | async-done | bytes 8388624 | tf_op jit(solution)/shard_map/all_gather | solution.py:120
  174.8 49.1 %all-gather.16.cloned.1.call-done = bf16[1,2048,2048]{2,1,0:T(8,128)(2,1)} async-done(((bf16[1,2048,512]{2,1,0:T(8,128)(2,1)}), bf16[1,2048,2048]{2,1,0:T(8,128)(2,1)}) %all-gather.16.cloned.1.call-update) | async-done | bytes 8388624 | tf_op jit(solution)/shard_map/all_gather | solution.py:120
  254.5 7.2 bitcast_dynamic-update-slice_fusion.4
  266.7 25.9 %reduce-scatter.18.cloned.1.call-done = bf16[64,2048]{1,0:T(8,128)(2,1)} async-done(((bf16[256,2048]{1,0:T(8,128)(2,1)}), bf16[64,2048]{1,0:T(8,128)(2,1)}) %reduce-scatter.18.cloned.1.call-update) | async-done | bytes 262160 | tf_op jit(solution)/shard_map/reduce_scatter | solution.py:72
  341.2 7.1 collective-permute-done.12
  348.4 7.5 bitcast_dynamic-update-slice_fusion.3
  360.8 31.2 %reduce-scatter.20.cloned.1.call-done = bf16[64,2048]{1,0:T(8,128)(2,1)} async-done(((bf16[256,2048]{1,0:T(8,128)(2,1)}), bf16[64,2048]{1,0:T(8,128)(2,1)}) %reduce-scatter.20.cloned.1.call-update) | async-done | bytes 262160 | tf_op jit(solution)/shard_map/reduce_scatter | solution.py:72
  436.2 7.2 collective-permute-done.19
  443.5 7.5 bitcast_dynamic-update-slice_fusion.2
  465.6 30.5 %reduce-scatter.22.cloned.1.call-done = bf16[64,2048]{1,0:T(8,128)(2,1)} async-done(((bf16[256,2048]{1,0:T(8,128)(2,1)}), bf16[64,2048]{1,0:T(8,128)(2,1)}) %reduce-scatter.22.cloned.1.call-update) | async-done | bytes 262160 | tf_op jit(solution)/shard_map/reduce_scatter | solution.py:72
  561.6 7.4 bitcast_dynamic-update-slice_fusion.1
  570.4 6.9 fusion.132
  583.3 24.6 %reduce-scatter.24.cloned.1.call-done = bf16[64,2048]{1,0:T(8,128)(2,1)} async-done(((bf16[256,2048]{1,0:T(8,128)(2,1)}), bf16[64,2048]{1,0:T(8,128)(2,1)}) %reduce-scatter.24.cloned.1.call-update) | async-done | bytes 262160 | tf_op jit(solution)/shard_map/reduce_scatter | solution.py:72
  673.4 8.5 bitcast_dynamic-update-slice_fusion
  703.8 19.0 %reduce-scatter.28.cloned.1.call-done = bf16[64,2048]{1,0:T(8,128)(2,1)} async-done(((bf16[256,2048]{1,0:T(8,128)(2,1)}), bf16[64,2048]{1,0:T(8,128)(2,1)}) %reduce-scatter.28.cloned.1.call-update) | async-done | bytes 262160 | tf_op jit(solution)/shard_map/reduce_scatter | solution.py:72
  752.9 6.9 fusion.68
  759.8 8.9 reduce-scatter.30.cloned.1.call-done
  803.9 8.6 bitcast_dynamic-update-slice_fusion.13
  827.0 21.7 %reduce-scatter.32.cloned.1.call-done = bf16[64,2048]{1,0:T(8,128)(2,1)} async-done(((bf16[256,2048]{1,0:T(8,128)(2,1)}), bf16[64,2048]{1,0:T(8,128)(2,1)}) %reduce-scatter.32.cloned.1.call-update) | async-done | bytes 262160 | tf_op jit(solution)/shard_map/reduce_scatter | solution.py:72
  879.1 6.9 fusion.66
  886.1 8.8 reduce-scatter.34.cloned.1.call-done
  931.9 8.7 bitcast_dynamic-update-slice_fusion.12
  963.9 14.5 reduce-scatter.36.cloned.1.call-done
  1007.8 6.8 fusion.64
  1014.6 8.8 reduce-scatter.38.cloned.1.call-done
  1058.1 8.6 bitcast_dynamic-update-slice_fusion.11
  1089.5 13.8 reduce-scatter.40.cloned.1.call-done
  1133.5 6.8 fusion.62
  1140.3 8.6 reduce-scatter.42.cloned.1.call-done
  1176.9 7.6 collective-permute-done.52
  1185.2 8.6 bitcast_dynamic-update-slice_fusion.10
  1211.5 7.6 fusion.135
  1219.2 9.0 reduce-scatter.44.cloned.1.call-done
  1274.6 15.6 convolution_bitcast_fusion.1
  1331.9 8.4 add_convert_fusion.1
  1340.4 12.5 convolution_bitcast_fusion
  1396.1 40.2 %collective-permute-done.62 = bf16[512,2048]{1,0:T(8,128)(2,1)} collective-permute-done((bf16[512,2048]{1,0:T(8,128)(2,1)S(1)}, bf16[512,2048]{1,0:T(8,128)(2,1)}, u32[]{:S(2)}, u32[]{:S(2)}) %collective-permute-start.62) | collective-permute-done | bytes 2097184 | tf_op jit(solution)/shard_map/ppermute | solution.py:79
  1441.5 8.3 add_convert_fusion
  1452.6 31.0 %collective-permute-done.66 = bf16[512,2048]{1,0:T(8,128)(2,1)} collective-permute-done((bf16[512,2048]{1,0:T(8,128)(2,1)}, bf16[512,2048]{1,0:T(8,128)(2,1)}, u32[]{:S(2)}, u32[]{:S(2)}) %collective-permute-start.66) | collective-permute-done | bytes 2097184 | tf_op jit(solution)/shard_map/ppermute | solution.py:79
  1488.4 43.0 %collective-permute-done.63 = bf16[512,2048]{1,0:T(8,128)(2,1)} collective-permute-done((bf16[512,2048]{1,0:T(8,128)(2,1)S(1)}, bf16[512,2048]{1,0:T(8,128)(2,1)}, u32[]{:S(2)}, u32[]{:S(2)}) %collective-permute-start.63) | collective-permute-done | bytes 2097184 | tf_op jit(solution)/shard_map/ppermute | solution.py:79
  1539.9 36.4 %collective-permute-done.67 = bf16[512,2048]{1,0:T(8,128)(2,1)S(1)} collective-permute-done((bf16[512,2048]{1,0:T(8,128)(2,1)S(1)}, bf16[512,2048]{1,0:T(8,128)(2,1)S(1)}, u32[]{:S(2)}, u32[]{:S(2)}) %collective-permute-start.67) | collective-permute-done | bytes 2097184 | tf_op jit(solution)/shard_map/ppermute | solution.py:79
  1603.0 68.3 %reduce-scatter.50.cloned.1.call-done = bf16[512,1024]{1,0:T(8,128)(2,1)} async-done(((bf16[2048,1024]{1,0:T(8,128)(2,1)}), bf16[512,1024]{1,0:T(8,128)(2,1)}) %reduce-scatter.50.cloned.1.call-update) | async-done | bytes 1048592 | tf_op jit(solution)/shard_map/reduce_scatter | solution.py:104
  1676.2 11.8 maximum_convert_fusion
  1705.6 7.8 collective-permute-done.59
  1716.4 11.8 maximum_convert_fusion.1
  (1082 shorter events, 876.3 us)
Async XLA Ops:
  7.2 51.0 %all-gather.10.cloned.1.call-start = ((), (), s32[]{:S(2)}) async-start(), calls=%async_computation.36 | async-start | bytes 2621440 | tf_op jit(solution)/shard_map/all_gather | solution.py:119
  9.7 95.4 %all-gather.14.cloned.1.call-start = ((), (), s32[]{:S(2)}) async-start(), calls=%async_computation.38 | async-start | bytes 2621440 | tf_op jit(solution)/shard_map/all_gather | solution.py:119
  11.7 152.4 %all-gather.12.cloned.1.call-start = ((), (), s32[]{:S(2)}) async-start(), calls=%async_computation.37 | async-start | bytes 10485760 | tf_op jit(solution)/shard_map/all_gather | solution.py:120
  58.3 165.6 %all-gather.16.cloned.1.call-start = ((), (), s32[]{:S(2)}) async-start(), calls=%async_computation.39 | async-start | bytes 10485760 | tf_op jit(solution)/shard_map/all_gather | solution.py:120
  105.1 187.5 %reduce-scatter.18.cloned.1.call-start = ((), (), s32[]{:S(2)}) async-start(), calls=%async_computation.17 | async-start | bytes 1310720 | tf_op jit(solution)/shard_map/reduce_scatter | solution.py:72
  106.1 12.7 collective-permute-start
  106.2 12.7 collective-permute-start.1
  230.8 13.3 collective-permute-start.4
  266.6 125.4 %reduce-scatter.20.cloned.1.call-start = ((), (), s32[]{:S(2)}) async-start(), calls=%async_computation.18 | async-start | bytes 1310720 | tf_op jit(solution)/shard_map/reduce_scatter | solution.py:72
  360.7 135.3 %reduce-scatter.22.cloned.1.call-start = ((), (), s32[]{:S(2)}) async-start(), calls=%async_computation.19 | async-start | bytes 1310720 | tf_op jit(solution)/shard_map/reduce_scatter | solution.py:72
  455.8 152.1 %reduce-scatter.24.cloned.1.call-start = ((), (), s32[]{:S(2)}) async-start(), calls=%async_computation.20 | async-start | bytes 1310720 | tf_op jit(solution)/shard_map/reduce_scatter | solution.py:72
  464.5 201.5 %collective-permute-start.36 = (bf16[64,2048]{1,0:T(8,128)(2,1)}, bf16[64,2048]{1,0:T(8,128)(2,1)}, u32[]{:S(2)}, u32[]{:S(2)}) collective-permute-start(bf16[64,2048]{1,0:T(8,128)(2,1)} %collective-permute-done.34), channel_id=1, source_target_pairs={{0,4},{4,8},{8,12},{12,0},{1,5},{5,9},{9,13},{13,1},{2,6},{6,10},{... | collective-permute-start | bytes 786440 | tf_op jit(solution)/shard_map/ppermute | solution.py:26
  510.3 11.9 collective-permute-start.22
  543.8 14.4 collective-permute-start.25
  577.3 145.5 %reduce-scatter.28.cloned.1.call-start = ((), (), s32[]{:S(2)}) async-start(), calls=%async_computation.22 | async-start | bytes 1310720 | tf_op jit(solution)/shard_map/reduce_scatter | solution.py:72
  621.0 12.5 collective-permute-start.29
  659.9 12.4 collective-permute-start.33
  694.4 74.2 %reduce-scatter.30.cloned.1.call-start = ((), (), s32[]{:S(2)}) async-start(), calls=%async_computation.23 | async-start | bytes 163840 | tf_op jit(solution)/shard_map/reduce_scatter | solution.py:72
  752.8 95.9 %reduce-scatter.32.cloned.1.call-start = ((), (), s32[]{:S(2)}) async-start(), calls=%async_computation.24 | async-start | bytes 1310720 | tf_op jit(solution)/shard_map/reduce_scatter | solution.py:72
  819.4 75.6 %reduce-scatter.34.cloned.1.call-start = ((), (), s32[]{:S(2)}) async-start(), calls=%async_computation.25 | async-start | bytes 163840 | tf_op jit(solution)/shard_map/reduce_scatter | solution.py:72
  879.1 99.3 %reduce-scatter.36.cloned.1.call-start = ((), (), s32[]{:S(2)}) async-start(), calls=%async_computation.26 | async-start | bytes 1310720 | tf_op jit(solution)/shard_map/reduce_scatter | solution.py:72
  911.0 12.9 collective-permute-start.42
  947.3 76.2 %reduce-scatter.38.cloned.1.call-start = ((), (), s32[]{:S(2)}) async-start(), calls=%async_computation.27 | async-start | bytes 163840 | tf_op jit(solution)/shard_map/reduce_scatter | solution.py:72
  1007.6 95.7 %reduce-scatter.40.cloned.1.call-start = ((), (), s32[]{:S(2)}) async-start(), calls=%async_computation.28 | async-start | bytes 1310720 | tf_op jit(solution)/shard_map/reduce_scatter | solution.py:72
  1073.5 75.4 %reduce-scatter.42.cloned.1.call-start = ((), (), s32[]{:S(2)}) async-start(), calls=%async_computation.29 | async-start | bytes 163840 | tf_op jit(solution)/shard_map/reduce_scatter | solution.py:72
  1133.0 95.1 %reduce-scatter.44.cloned.1.call-start = ((), (), s32[]{:S(2)}) async-start(), calls=%async_computation.30 | async-start | bytes 1310720 | tf_op jit(solution)/shard_map/reduce_scatter | solution.py:72
  1200.6 123.6 %reduce-scatter.46.cloned.1.call-start = ((), (), s32[]{:S(2)}) async-start(), calls=%async_computation.31 | async-start | bytes 163840 | tf_op jit(solution)/shard_map/reduce_scatter | solution.py:72
  1250.7 199.2 %reduce-scatter.26.cloned.1.call-start = ((), (), s32[]{:S(2)}) async-start(), calls=%async_computation.21 | async-start | bytes 1310720 | tf_op jit(solution)/shard_map/reduce_scatter | solution.py:72
  1254.9 330.5 %all-reduce.4.cloned.1.call-start = ((), (), s32[]{:S(2)}) async-start(), calls=%async_computation.32 | async-start | bytes 188416 | tf_op jit(solution)/shard_map/psum | solution.py:312
  1304.7 27.3 %collective-permute-start.53 = (bf16[1024,2048]{1,0:T(8,128)(2,1)}, bf16[1024,2048]{1,0:T(8,128)(2,1)}, u32[]{:S(2)}, u32[]{:S(2)}) collective-permute-start(bf16[1024,2048]{1,0:T(8,128)(2,1)} %dynamic-slice_convert_fusion.3), channel_id=1, source_target_pairs={{0,1},{1,0},{2,3},{3,2},{4,5},{5,4},{6,7},{7,6},{8,9},{9,8},{10,11... | collective-permute-start | bytes 12582920 | tf_op jit(solution)/shard_map/ppermute | solution.py:79
  1314.9 62.1 %collective-permute-start.61 = (bf16[1024,2048]{1,0:T(8,128)(2,1)}, bf16[1024,2048]{1,0:T(8,128)(2,1)}, u32[]{:S(2)}, u32[]{:S(2)}) collective-permute-start(bf16[1024,2048]{1,0:T(8,128)(2,1)} %dynamic-slice_convert_fusion.1), channel_id=1, source_target_pairs={{0,1},{1,0},{2,3},{3,2},{4,5},{5,4},{6,7},{7,6},{8,9},{9,8},{10,11... | collective-permute-start | bytes 12582920 | tf_op jit(solution)/shard_map/ppermute | solution.py:79
  1329.0 260.4 %all-reduce.6.cloned.1.call-start = ((), (), s32[]{:S(2)}) async-start(), calls=%async_computation.34 | async-start | bytes 2097152 | tf_op jit(solution)/shard_map/psum | solution.py:308
  1331.9 267.0 %reduce-scatter.48.cloned.1.call-start = ((), (), s32[]{:S(2)}) async-start(), calls=%async_computation.33 | async-start | bytes 5242880 | tf_op jit(solution)/shard_map/reduce_scatter | solution.py:104
  1340.4 330.9 %reduce-scatter.50.cloned.1.call-start = ((), (), s32[]{:S(2)}) async-start(), calls=%async_computation.35 | async-start | bytes 5242880 | tf_op jit(solution)/shard_map/reduce_scatter | solution.py:104
  1361.3 26.7 %collective-permute-start.65 = (bf16[1024,2048]{1,0:T(8,128)(2,1)}, bf16[1024,2048]{1,0:T(8,128)(2,1)}, u32[]{:S(2)}, u32[]{:S(2)}) collective-permute-start(bf16[1024,2048]{1,0:T(8,128)(2,1)} %dynamic-slice_convert_fusion), channel_id=1, source_target_pairs={{0,1},{1,0},{2,3},{3,2},{4,5},{5,4},{6,7},{7,6},{8,9},{9,8},{10,11... | collective-permute-start | bytes 12582920 | tf_op jit(solution)/shard_map/ppermute | solution.py:79
  1377.0 64.5 %collective-permute-start.57 = (bf16[2048,1024]{1,0:T(8,128)(2,1)}, bf16[2048,1024]{1,0:T(8,128)(2,1)}, u32[]{:S(2)}, u32[]{:S(2)}) collective-permute-start(bf16[2048,1024]{1,0:T(8,128)(2,1)} %dynamic-slice_convert_fusion.2), channel_id=1, source_target_pairs={{0,1},{1,0},{2,3},{3,2},{4,5},{5,4},{6,7},{7,6},{8,9},{9,8},{10,11... | collective-permute-start | bytes 12582920 | tf_op jit(solution)/shard_map/ppermute | solution.py:79
  1386.7 49.7 %collective-permute-start.62 = (bf16[512,2048]{1,0:T(8,128)(2,1)S(1)}, bf16[512,2048]{1,0:T(8,128)(2,1)}, u32[]{:S(2)}, u32[]{:S(2)}) collective-permute-start(bf16[512,2048]{1,0:T(8,128)(2,1)S(1)} %dynamic-slice_convert_fusion.5), channel_id=1, source_target_pairs={{0,2},{1,3},{2,0},{3,1},{4,6},{5,7},{6,4},{7,5},{8,10},{9,11},{10,... | collective-permute-start | bytes 6291464 | tf_op jit(solution)/shard_map/ppermute | solution.py:79
  1396.0 87.6 %collective-permute-start.66 = (bf16[512,2048]{1,0:T(8,128)(2,1)}, bf16[512,2048]{1,0:T(8,128)(2,1)}, u32[]{:S(2)}, u32[]{:S(2)}) collective-permute-start(bf16[512,2048]{1,0:T(8,128)(2,1)} %dynamic-slice_convert_fusion.4), channel_id=1, source_target_pairs={{0,2},{1,3},{2,0},{3,1},{4,6},{5,7},{6,4},{7,5},{8,10},{9,11},{10,... | collective-permute-start | bytes 6291464 | tf_op jit(solution)/shard_map/ppermute | solution.py:79
  1439.9 91.5 %collective-permute-start.63 = (bf16[512,2048]{1,0:T(8,128)(2,1)S(1)}, bf16[512,2048]{1,0:T(8,128)(2,1)}, u32[]{:S(2)}, u32[]{:S(2)}) collective-permute-start(bf16[512,2048]{1,0:T(8,128)(2,1)S(1)} %add_convert_fusion.3), channel_id=1, source_target_pairs={{0,2},{1,3},{2,0},{3,1},{4,6},{5,7},{6,4},{7,5},{8,10},{9,11},{10,... | collective-permute-start | bytes 6291464 | tf_op jit(solution)/shard_map/ppermute | solution.py:79
  1487.1 89.2 %collective-permute-start.67 = (bf16[512,2048]{1,0:T(8,128)(2,1)S(1)}, bf16[512,2048]{1,0:T(8,128)(2,1)S(1)}, u32[]{:S(2)}, u32[]{:S(2)}) collective-permute-start(bf16[512,2048]{1,0:T(8,128)(2,1)S(1)} %add_convert_fusion.2), channel_id=1, source_target_pairs={{0,2},{1,3},{2,0},{3,1},{4,6},{5,7},{6,4},{7,5},{8,10},{9,11},{10,... | collective-permute-start | bytes 6291464 | tf_op jit(solution)/shard_map/ppermute | solution.py:79
  1536.8 55.5 %collective-permute-start.64 = (bf16[1024,2048]{1,0:T(8,128)(2,1)}, bf16[1024,2048]{1,0:T(8,128)(2,1)}, u32[]{:S(2)}, u32[]{:S(2)}) collective-permute-start(bf16[1024,2048]{1,0:T(8,128)(2,1)} %pad_maximum_fusion), channel_id=1, source_target_pairs={{0,1},{1,0},{2,3},{3,2},{4,5},{5,4},{6,7},{7,6},{8,9},{9,8},{10,11... | collective-permute-start | bytes 12582920 | tf_op jit(solution)/shard_map/ppermute | solution.py:79
  1579.6 113.1 %collective-permute-start.68 = (bf16[1024,2048]{1,0:T(8,128)(2,1)}, bf16[1024,2048]{1,0:T(8,128)(2,1)}, u32[]{:S(2)}, u32[]{:S(2)}) collective-permute-start(bf16[1024,2048]{1,0:T(8,128)(2,1)} %pad_maximum_fusion.1), channel_id=1, source_target_pairs={{0,1},{1,0},{2,3},{3,2},{4,5},{5,4},{6,7},{7,6},{8,9},{9,8},{10,11... | collective-permute-start | bytes 12582920 | tf_op jit(solution)/shard_map/ppermute | solution.py:79
  1601.7 86.3 %collective-permute-start.54 = (bf16[512,512]{1,0:T(8,128)(2,1)S(1)}, bf16[512,512]{1,0:T(8,128)(2,1)S(1)}, u32[]{:S(2)}, u32[]{:S(2)}) collective-permute-start(bf16[512,512]{1,0:T(8,128)(2,1)S(1)} %dynamic-slice_convert_fusion.7), channel_id=1, source_target_pairs={{0,2},{1,3},{2,0},{3,1},{4,6},{5,7},{6,4},{7,5},{8,10},{9,11},{10,... | collective-permute-start | bytes 1572872 | tf_op jit(solution)/shard_map/ppermute | solution.py:79
  1675.0 14.9 collective-permute-start.58
  1689.5 12.6 collective-permute-start.55
  1691.4 21.9 %collective-permute-start.59 = (bf16[512,512]{1,0:T(8,128)(2,1)S(1)}, bf16[512,512]{1,0:T(8,128)(2,1)S(1)}, u32[]{:S(2)}, u32[]{:S(2)}) collective-permute-start(bf16[512,512]{1,0:T(8,128)(2,1)S(1)} %add_convert_fusion.4), channel_id=1, source_target_pairs={{0,2},{1,3},{2,0},{3,1},{4,6},{5,7},{6,4},{7,5},{8,10},{9,11},{10,... | collective-permute-start | bytes 1572872 | tf_op jit(solution)/shard_map/ppermute | solution.py:79
  1702.3 25.9 %collective-permute-start.56 = (bf16[1024,512]{1,0:T(8,128)(2,1)S(1)}, bf16[1024,512]{1,0:T(8,128)(2,1)}, u32[]{:S(2)}, u32[]{:S(2)}) collective-permute-start(bf16[1024,512]{1,0:T(8,128)(2,1)S(1)} %pad_maximum_fusion.3), channel_id=1, source_target_pairs={{0,1},{1,0},{2,3},{3,2},{4,5},{5,4},{6,7},{7,6},{8,9},{9,8},{10,11... | collective-permute-start | bytes 3145736 | tf_op jit(solution)/shard_map/ppermute | solution.py:79
  1714.6 17.9 %collective-permute-start.60 = (bf16[512,1024]{1,0:T(8,128)(2,1)}, bf16[512,1024]{1,0:T(8,128)(2,1)}, u32[]{:S(2)}, u32[]{:S(2)}) collective-permute-start(bf16[512,1024]{1,0:T(8,128)(2,1)} %pad_maximum_fusion.4), channel_id=1, source_target_pairs={{0,1},{1,0},{2,3},{3,2},{4,5},{5,4},{6,7},{7,6},{8,9},{9,8},{10,11... | collective-permute-start | bytes 3145736 | tf_op jit(solution)/shard_map/ppermute | solution.py:79
  (257 other events, 4176.9 us)
Sparse Core Ops, SparseCore 0:
  10.2 47.9 all-gather.9
  60.4 44.6 all-gather.13
  106.7 57.4 all-gather.11
  165.5 58.2 all-gather.15
  266.7 25.8 reduce-scatter.17
  360.9 31.0 reduce-scatter.19
  455.9 40.0 reduce-scatter.21
  577.4 30.4 reduce-scatter.23
  694.6 28.2 reduce-scatter.27
  752.9 15.6 reduce-scatter.29
  819.5 29.1 reduce-scatter.31
  879.2 15.6 reduce-scatter.33
  947.4 30.9 reduce-scatter.35
  1007.7 15.6 reduce-scatter.37
  1073.6 29.6 reduce-scatter.39
  1133.2 15.7 reduce-scatter.41
  1200.8 27.3 reduce-scatter.43
  1250.8 15.7 reduce-scatter.45
  1268.9 27.4 reduce-scatter.25
  1329.2 85.1 all-reduce.3
  1417.8 93.6 all-reduce.5
  1514.3 76.5 reduce-scatter.47
  1594.0 77.2 reduce-scatter.49
